TPU v7x, 512 devices: a whole 4x4x16 slice. The times are simulated.
512 devices in a mesh: grp: 32 (over y, z_lo), tp: 16 (over z_hi, x, core).
Axes of the slice: x: 4, y: 4, z: 16 (z_hi: 2, z_lo: 8; z = z_hi * 8 + z_lo), core: 2. Of those that a mesh axis runs over, the one named last changes fastest.
Arguments:
- tokens: bfloat16 [65536, 1536], P(('grp', 'tp')), may hold values from -6 to 6
- attn_gain: float32 [1536], replicated, may hold values from 0.1 to 1.9
- ffn_gain: float32 [1536], replicated, may hold values from 0.1 to 1.9
- w_query: bfloat16 [1536, 1024], P(None, 'tp')
- key_value_weight: bfloat16 [1536, 1024], P(None, 'tp'), may hold values from -0.15625 to 0.15625
- w_out: bfloat16 [1024, 1536], P('tp'), may hold values from -0.1875 to 0.1875
- segment_ids: int32 [65536], P(('grp', 'tp')), may hold values from 0 to 65535, as said below
- expert_ids: int32 [65536, 2], P(('grp', 'tp')), may hold values from 0 to 7, all different within a row; in each aligned block of 128 rows (0 to 127, 128 to 255, ...) at most 48 rows name the same one
- route_weights: float32 [65536, 2], P(('grp', 'tp')), may hold values from 0.2 to 1
- w_gate: bfloat16 [1536, 4096], P(None, 'tp'), may hold values from -0.15625 to 0.15625
- w_up: bfloat16 [1536, 4096], P(None, 'tp'), may hold values from -0.15625 to 0.15625
- w_down: bfloat16 [4096, 1536], P('tp'), may hold values from -0.25 to 0.25
- page_table: int32 [32, 128], P('grp'), may hold values from 0 to 127, each once within a row
Outputs:
- hidden_out: bfloat16 [65536, 1536], P(('grp', 'tp'))
- kv_cache: bfloat16 [4096, 16, 1024], P(('grp', 'tp'))
Inputs may be any that keep to these rules, and one draw needn't show every extreme that they name: `segment_ids`: each token's number is the stream position of its prompt's first token, so numbers never fall along the stream; a prompt covers at most 1024 tokens and some prompt exactly 1024; a prompt runs from every group into the next; the last token of the stream is a prompt of its own. `expert_ids`: in the tokens of one device no expert is named more than 48 times; in some device's tokens one expert is named exactly 48 times. `page_table`: each row names every page of the group once.
All inputs are finite; a program needn't handle non-finite values.
Results may differ from a plain program's by a relative error of at most 0.015.
The roundings to bfloat16 on the way count: a program that leaves them out, or rounds other values in their place, can miss the bound.
Values may be sent and summed in bfloat16 or wider, within the bound.
No kernel may reach another device: no remote copies, remote signals or barrier semaphores. Data moves between devices by JAX's collectives and lax.ppermute only.
A program may use at most 64 MiB of HBM per device.

v0:
```python
import jax
import jax.numpy as jnp
from jax import lax
from jax.sharding import PartitionSpec as P

HEAD_SIZE = 64
PAGE = 16


def partner_2(block, axis, bit):
    count = lax.axis_size(axis)
    route = []
    for low in range(count):
        high = low | 1 << bit
        if high != low and high < count:
            route += [(low, high), (high, low)]
    return lax.ppermute(block, axis, route)


def from_behind(block, axis, distance):
    devices = range(lax.axis_size(axis))
    route = [(i - distance, i) for i in devices if i - distance in devices]
    return lax.ppermute(block, axis, route)


def rms_scale(row_data, gain_vec):
    values = row_data.astype(jnp.float32)
    inverse = lax.rsqrt(jnp.mean(values * values, axis=-1, keepdims=True) + 1e-05)
    return (values * inverse * gain_vec).astype(jnp.bfloat16)


def attend_blocks(query_rows, key_cat, value_cat, seg_query, seg_cat, maxlen, offset, block_rows):
    group_tok = query_rows.shape[0]
    key_span = maxlen + block_rows

    def one_block(block_index):
        first_row = block_index * block_rows
        query_block = lax.dynamic_slice_in_dim(query_rows, first_row, block_rows, 0)
        seg_block = lax.dynamic_slice_in_dim(seg_query, first_row, block_rows, 0)
        key_block = lax.dynamic_slice_in_dim(key_cat, first_row + offset, key_span, 0)
        value_block = lax.dynamic_slice_in_dim(value_cat, first_row + offset, key_span, 0)
        seg_keys = lax.dynamic_slice_in_dim(seg_cat, first_row + offset, key_span, 0)
        key_pos = first_row - maxlen + jnp.arange(key_span, dtype=jnp.int32)
        query_pos = first_row + jnp.arange(block_rows, dtype=jnp.int32)
        scores = (
            jnp.einsum("qhd,khd->hqk", query_block, key_block, preferred_element_type=jnp.float32)
            * 0.125
        )
        allowed = (seg_block[:, None] == seg_keys[None, :]) & (
            key_pos[None, :] <= query_pos[:, None]
        )
        scores = jnp.where(allowed[None], scores, -1e30)
        row_max = jnp.max(scores, axis=-1, keepdims=True)
        exponent = jnp.exp(scores - row_max)
        attention = (exponent / jnp.sum(exponent, axis=-1, keepdims=True)).astype(jnp.bfloat16)
        result = jnp.einsum(
            "hqk,khd->qhd", attention, value_block, preferred_element_type=jnp.float32
        )
        return result.astype(jnp.bfloat16)

    blocks = lax.map(one_block, jnp.arange(group_tok // block_rows, dtype=jnp.int32))
    return blocks.reshape(group_tok, -1)


def body(
    tokens,
    attn_gain,
    ffn_gain,
    w_query,
    key_value_weight,
    w_out,
    segment_ids,
    expert_ids,
    route_weights,
    w_gate,
    w_up,
    w_down,
    page_table,
):
    tok_rows = tokens.shape[0]
    tp_size = lax.axis_size("tp")
    head_cols = w_query.shape[1]
    heads_here = head_cols // HEAD_SIZE
    normed_in = rms_scale(tokens, attn_gain)
    both_cols = jnp.concatenate([w_query, key_value_weight], axis=1)
    projected = jnp.dot(
        lax.all_gather(normed_in, "tp", axis=0, tiled=True),
        both_cols,
        preferred_element_type=jnp.float32,
    ).astype(jnp.bfloat16)
    group_tok = projected.shape[0]
    query_rows = projected[:, :head_cols].reshape(group_tok, heads_here, HEAD_SIZE)
    own_slice = projected[:, head_cols:]
    page_count = group_tok // PAGE
    page_order = page_table[0]
    page_ids = jnp.arange(page_count, dtype=jnp.int32)
    source_block = jnp.sum(
        jnp.where(page_order[None, :] == page_ids[:, None], page_ids[None, :], 0), axis=1
    )
    ordered_pages = own_slice.reshape(page_count, PAGE, head_cols)[source_block]
    kv_cache = lax.all_to_all(ordered_pages, "tp", split_axis=0, concat_axis=2, tiled=True)
    seg_all = lax.all_gather(segment_ids, "tp", axis=0, tiled=True)
    maxlen = group_tok // 2
    block_rows = min(512, group_tok)
    low_half = lax.axis_index("tp") < tp_size // 2
    pair_bit = tp_size.bit_length() - 2
    partner = partner_2(own_slice, "tp", pair_bit)
    key_rows = jnp.where(low_half, own_slice, partner)
    value_rows = jnp.where(low_half, partner, own_slice)
    tail_keys, tail_values, tail_seg = from_behind((key_rows, value_rows, seg_all), "grp", 1)
    tail_seg = jnp.where(lax.axis_index("grp") > 0, tail_seg, -1)
    key_cat = jnp.concatenate([tail_keys, key_rows], 0).reshape(-1, heads_here, HEAD_SIZE)
    value_cat = jnp.concatenate([tail_values, value_rows], 0).reshape(-1, heads_here, HEAD_SIZE)
    seg_cat = jnp.concatenate([tail_seg, seg_all], 0)
    attended = attend_blocks(
        query_rows, key_cat, value_cat, seg_all, seg_cat, maxlen, group_tok - maxlen, block_rows
    )
    token_heads = lax.all_to_all(attended, "tp", split_axis=0, concat_axis=1, tiled=True)
    out_sum = jnp.dot(
        token_heads,
        lax.all_gather(w_out, "tp", axis=0, tiled=True),
        preferred_element_type=jnp.float32,
    )
    mid_state = (tokens.astype(jnp.float32) + out_sum).astype(jnp.bfloat16)
    normed_mid = rms_scale(mid_state, ffn_gain)
    expert_count = tp_size // 2
    choice_count = expert_ids.shape[1]
    capacity = min(tok_rows, 3 * tok_rows * choice_count // (2 * expert_count))
    routes_flat = expert_ids.reshape(-1)
    onehot = (routes_flat[:, None] == jnp.arange(expert_count, dtype=jnp.int32)[None, :]).astype(
        jnp.int32
    )
    earlier = jnp.cumsum(onehot, axis=0) - onehot
    slot_index = jnp.sum(earlier * onehot, axis=-1)
    target_slot = routes_flat * capacity + slot_index
    placement_map = (
        target_slot[:, None] == jnp.arange(expert_count * capacity, dtype=jnp.int32)[None, :]
    )
    placement_map = placement_map.reshape(tok_rows, choice_count, expert_count * capacity)
    select_map = jnp.sum(placement_map.astype(jnp.int32), axis=1).astype(jnp.bfloat16)
    model_width = normed_mid.shape[1]
    buffers = jnp.einsum(
        "te,td->ed", select_map, normed_mid, preferred_element_type=jnp.float32
    ).astype(jnp.bfloat16)
    send_buf = jnp.broadcast_to(
        buffers.reshape(expert_count, 1, capacity, model_width),
        (expert_count, 2, capacity, model_width),
    )
    send_buf = send_buf.reshape(2 * expert_count, capacity, model_width)
    row_data = lax.all_to_all(send_buf, "tp", split_axis=0, concat_axis=0, tiled=True)
    slot_count = row_data.shape[1]
    flat_rows = row_data.reshape(-1, model_width)
    gate_act = jnp.dot(flat_rows, w_gate, preferred_element_type=jnp.float32)
    up_act = jnp.dot(flat_rows, w_up, preferred_element_type=jnp.float32)
    activated = (jax.nn.silu(gate_act) * up_act).astype(jnp.bfloat16)
    half_out = jnp.dot(activated, w_down, preferred_element_type=jnp.float32).astype(jnp.bfloat16)
    half_out = half_out.reshape(row_data.shape[0], slot_count, model_width)
    returned = lax.all_to_all(half_out, "tp", split_axis=0, concat_axis=0, tiled=True)
    halves = returned.reshape(expert_count, 2, capacity, model_width)
    summed = (halves[:, 0].astype(jnp.float32) + halves[:, 1].astype(jnp.float32)).reshape(
        expert_count * capacity, model_width
    )
    picked = summed[target_slot].reshape(tok_rows, choice_count, model_width)
    expert_sum = jnp.sum(picked * route_weights[..., None], axis=1)
    hidden_out = (mid_state.astype(jnp.float32) + expert_sum).astype(jnp.bfloat16)
    return (hidden_out, kv_cache)


def solution(mesh):
    in_specs = (
        P(("grp", "tp"), None),
        P(),
        P(),
        P(None, "tp"),
        P(None, "tp"),
        P("tp", None),
        P(("grp", "tp")),
        P(("grp", "tp"), None),
        P(("grp", "tp"), None),
        P(None, "tp"),
        P(None, "tp"),
        P("tp", None),
        P("grp", None),
    )
    out_specs = (P(("grp", "tp"), None), P(("grp", "tp"), None, None))
    return jax.shard_map(body, mesh=mesh, in_specs=in_specs, out_specs=out_specs, check_vma=False)
```

profile of v0, /device:TPU:103, one launch (start us, length us, event | category | flops | bytes accessed | tf_op | source)
XLA Modules:
  0.0 620.0 jit_solution(16437475761888153532)
XLA Ops:
  7.2 1.2 fusion.17
  8.5 1.9 fusion.19
  10.4 152.5 %all-gather.4.cloned.1.call-done = bf16[2048,1536]{1,0:T(8,128)(2,1)} async-done(((bf16[128,1536]{1,0:T(8,128)(2,1)}), bf16[2048,1536]{1,0:T(8,128)(2,1)}) %all-gather.4.cloned.1.call-update) | async-done | bytes 6291472 | tf_op jit(solution)/shard_map/all_gather | solution.py:87
  163.0 4.9 convolution_convert_fusion.2
  167.9 1.9 collective-permute-start
  169.9 43.4 %all-gather = s32[16,1,128]{2,1,0:T(1,128)S(1)} all-gather(s32[1,1,128]{2,1,0:T(1,128)S(1)} %bitcast.102), channel_id=1, replica_groups=mesh['grp'=32,'tp'=16] {'tp'}, dimensions={0}, use_global_device_ids=true | all-gather | bytes 8704 | tf_op jit(solution)/shard_map/all_gather | solution.py:102
  213.2 1.9 collective-permute-start.2
  215.3 1.9 collective-permute-start.3
  217.2 3.0 collective-permute-done.2
  220.2 1.9 collective-permute-start.1
  222.1 5.5 collective-permute-done.3
  227.7 5.6 collective-permute-done.1
  233.4 15.4 %while.12 = (s32[]{:T(128)}, bf16[4,512,1,64]{1,3,2,0:T(8,128)(2,1)S(1)}, s32[4]{0:T(128)S(1)}, bf16[4096,1,64]{0,2,1:T(8,128)(2,1)S(1)}, s32[2048]{0:T(1024)S(1...) while((s32[]{:T(128)}, ...), condition=%wide.region_4.5_spmd, body=%wide.region_1.4_spmd.sunk | while | flops 210011136 | bytes 10017057 | solution.py:61
  233.4 0.6 dynamic_slice.62
  234.8 1.0 fusion.54
  236.4 0.8 fusion.56
  238.6 1.0 fusion.54
  240.2 0.8 fusion.56
  242.5 1.0 fusion.54
  244.1 0.8 fusion.56
  246.3 1.0 fusion.54
  247.9 0.8 fusion.56
  249.1 0.8 copy.44
  249.9 20.4 %all-to-all-start = ((bf16[16,128,64]{1,2,0:T(8,128)(2,1)}), bf16[16,128,64]{1,2,0:T(8,128)(2,1)S(1)}, u32[]{:S(2)}, u32[]{:S(2)}) async-start(bf16[16,128,64]{1,2,0:T(8,128)(2,1)} %copy.44), calls=%async_computation | async-start | bytes 524288 | tf_op jit(solution)/shard_map/all_to_all | solution.py:118
  271.9 55.3 %all-gather.6.cloned.1.call-done = bf16[1024,1536]{1,0:T(8,128)(2,1)} async-done(((bf16[64,1536]{1,0:T(8,128)(2,1)}), bf16[1024,1536]{1,0:T(8,128)(2,1)}) %all-gather.6.cloned.1.call-update) | async-done | bytes 3145744 | tf_op jit(solution)/shard_map/all_gather | solution.py:121
  327.2 2.6 multiply_reduce_fusion.1
  329.8 0.9 copy-done.2
  331.2 1.6 broadcast_in_dim.43
  332.9 6.5 %all-to-all-start.1 = ((bf16[16,48,1536]{2,1,0:T(8,128)(2,1)}), bf16[16,48,1536]{2,1,0:T(8,128)(2,1)S(1)}, u32[]{:S(2)}, u32[]{:S(2)}) async-start(bf16[16,48,1536]{2,1,0:T(8,128)(2,1)} %bitcast.17), calls=%async_computation.1 | async-start | bytes 4718592 | tf_op jit(solution)/shard_map/all_to_all | solution.py:150
  339.5 1.0 copy.52
  340.5 2.5 gather_fusion.1
  343.0 2.1 reshape.219
  345.2 109.4 %all-to-all-done.1 = bf16[16,48,1536]{2,1,0:T(8,128)(2,1)S(1)} async-done(((bf16[16,48,1536]{2,1,0:T(8,128)(2,1)}), bf16[16,48,1536]{2,1,0:T(8,128)(2,1)S(1)}, u32[]{:S(2)}, u32[]{:S(2)}) %all-to-all-start.1) | async-done | bytes 2359328 | tf_op jit(solution)/shard_map/all_to_all | solution.py:150
  454.6 10.4 %all-to-all-start.3 = ((bf16[16,2,4096]{2,1,0:T(2,128)(2,1)}), bf16[16,2,4096]{2,1,0:T(2,128)(2,1)S(1)}, u32[]{:S(2)}, u32[]{:S(2)}) async-start(bf16[16,2,4096]{2,1,0:T(2,128)(2,1)} %reshape.219), calls=%async_computation.3 | async-start | bytes 524288 | tf_op jit(solution)/shard_map/all_to_all | solution.py:101
  465.0 2.8 fusion.40
  467.8 5.3 convolution_convert_fusion
  473.1 85.0 %all-to-all-done.3 = bf16[16,2,4096]{2,1,0:T(2,128)(2,1)S(1)} async-done(((bf16[16,2,4096]{2,1,0:T(2,128)(2,1)}), bf16[16,2,4096]{2,1,0:T(2,128)(2,1)S(1)}, u32[]{:S(2)}, u32[]{:S(2)}) %all-to-all-start.3) | async-done | bytes 262176 | tf_op jit(solution)/shard_map/all_to_all | solution.py:101
  558.1 4.5 all-to-all-start.2
  563.0 1.2 reshape.220
  564.1 2.2 copy.53
  566.3 2.1 all_to_all.42
  568.5 33.7 %all-to-all-done.2 = bf16[16,48,1536]{2,1,0:T(8,128)(2,1)S(1)} async-done(((bf16[16,48,1536]{2,1,0:T(8,128)(2,1)}), bf16[16,48,1536]{2,1,0:T(8,128)(2,1)S(1)}, u32[]{:S(2)}, u32[]{:S(2)}) %all-to-all-start.2) | async-done | bytes 2359328 | tf_op jit(solution)/shard_map/all_to_all | solution.py:158
  602.2 1.4 copy-done.1
  603.6 1.9 convert_add_fusion
  605.5 2.3 gather_fusion
  607.9 2.3 reshape.198
  610.2 2.2 multiply_reduce_fusion
  612.4 0.8 add_convert_fusion
  (80 shorter events, 7.9 us)
Async XLA Ops:
  7.2 460.7 %copy-start = (bf16[256,1536]{1,0:T(8,128)(2,1)S(1)}, bf16[256,1536]{1,0:T(8,128)(2,1)}, u32[]{:S(2)}) copy-start(bf16[256,1536]{1,0:T(8,128)(2,1)} %param.26) | copy-start | bytes 2359300
  7.2 155.8 %all-gather.4.cloned.1.call-start = ((), (), s32[]{:S(2)}) async-start(), calls=%async_computation.4 | async-start | bytes 6684672 | tf_op jit(solution)/shard_map/all_gather | solution.py:87
  10.4 159.5 %copy-start.8 = (s32[128]{0:T(128)S(1)}, s32[128]{0:T(128)}, u32[]{:S(2)}) copy-start(s32[128]{0:T(128)} %param.21) | copy-start | bytes 1540
  10.4 316.8 %all-gather.6.cloned.1.call-start = ((), (), s32[]{:S(2)}) async-start(), calls=%async_computation.5 | async-start | bytes 3342336 | tf_op jit(solution)/shard_map/all_gather | solution.py:121
  167.9 47.3 %collective-permute-start = (bf16[2048,64]{0,1:T(8,128)(2,1)S(1)}, bf16[2048,64]{0,1:T(8,128)(2,1)S(1)}, u32[]{:S(2)}, u32[]{:S(2)}) collective-permute-start(bf16[2048,64]{0,1:T(8,128)(2,1)S(1)} %slice.28), channel_id=1, source_target_pairs={{0,8},{8,0},{1,9},{9,1},{2,10},{10,2},{3,11},{11,3},{4,12},{12,4},... | collective-permute-start | bytes 786440 | tf_op jit(solution)/shard_map/ppermute | solution.py:17
  213.2 7.0 %collective-permute-start.2 = (s32[2048]{0:T(1024)S(1)}, s32[2048]{0:T(1024)S(1)}, u32[]{:S(2)}, u32[]{:S(2)}) collective-permute-start(s32[2048]{0:T(1024)S(1)} %bitcast.97), channel_id=1, source_target_pairs={{0,16},{16,32},{32,48},{48,64},{64,80},{80,96},{96,112},{112,128},... | collective-permute-start | bytes 24584 | tf_op jit(solution)/shard_map/ppermute | solution.py:23
  215.3 12.4 %collective-permute-start.3 = (bf16[2048,64]{0,1:T(8,128)(2,1)S(1)}, bf16[2048,64]{0,1:T(8,128)(2,1)S(1)}, u32[]{:S(2)}, u32[]{:S(2)}) collective-permute-start(bf16[2048,64]{0,1:T(8,128)(2,1)S(1)} %get-tuple-element.131), channel_id=1, source_target_pairs={{0,16},{16,32},{32,48},{48,64},{64,80},{80,96},{96,112},{112,128},... | collective-permute-start | bytes 786440 | tf_op jit(solution)/shard_map/ppermute | solution.py:23
  220.2 13.1 %collective-permute-start.1 = (bf16[2048,64]{0,1:T(8,128)(2,1)S(1)}, bf16[2048,64]{0,1:T(8,128)(2,1)S(1)}, u32[]{:S(2)}, u32[]{:S(2)}) collective-permute-start(bf16[2048,64]{0,1:T(8,128)(2,1)S(1)} %get-tuple-element.132), channel_id=1, source_target_pairs={{0,16},{16,32},{32,48},{48,64},{64,80},{80,96},{96,112},{112,128},... | collective-permute-start | bytes 786440 | tf_op jit(solution)/shard_map/ppermute | solution.py:23
  233.3 36.9 %copy-start.6 = (s32[128,2]{0,1:T(2,128)S(1)}, s32[128,2]{0,1:T(2,128)}, u32[]{:S(2)}) copy-start(s32[128,2]{0,1:T(2,128)} %param.22) | copy-start | bytes 3076
  248.8 78.4 %copy-start.4 = (bf16[128,1536]{1,0:T(8,128)(2,1)S(1)}, bf16[128,1536]{1,0:T(8,128)(2,1)}, u32[]{:S(2)}) copy-start(bf16[128,1536]{1,0:T(8,128)(2,1)} %param.15) | copy-start | bytes 1179652
  249.9 77.3 %all-to-all-start = ((bf16[16,128,64]{1,2,0:T(8,128)(2,1)}), bf16[16,128,64]{1,2,0:T(8,128)(2,1)S(1)}, u32[]{:S(2)}, u32[]{:S(2)}) async-start(bf16[16,128,64]{1,2,0:T(8,128)(2,1)} %copy.44), calls=%async_computation | async-start | bytes 524288 | tf_op jit(solution)/shard_map/all_to_all | solution.py:118
  271.8 58.9 %copy-start.5 = (f32[1536]{0:T(1024)S(1)}, f32[1536]{0:T(1024)}, u32[]{:S(2)}) copy-start(f32[1536]{0:T(1024)} %param.17) | copy-start | bytes 18436
  329.8 0.9 copy-start.2
  332.9 6.5 %copy-start.9 = (s32[1,128]{1,0:T(1,128)S(1)}, s32[1,128]{1,0:T(1,128)}, u32[]{:S(2)}) copy-start(s32[1,128]{1,0:T(1,128)} %param.27) | copy-start | bytes 1540
  332.9 121.7 %all-to-all-start.1 = ((bf16[16,48,1536]{2,1,0:T(8,128)(2,1)}), bf16[16,48,1536]{2,1,0:T(8,128)(2,1)S(1)}, u32[]{:S(2)}, u32[]{:S(2)}) async-start(bf16[16,48,1536]{2,1,0:T(8,128)(2,1)} %bitcast.17), calls=%async_computation.1 | async-start | bytes 4718592 | tf_op jit(solution)/shard_map/all_to_all | solution.py:150
  454.6 103.5 %all-to-all-start.3 = ((bf16[16,2,4096]{2,1,0:T(2,128)(2,1)}), bf16[16,2,4096]{2,1,0:T(2,128)(2,1)S(1)}, u32[]{:S(2)}, u32[]{:S(2)}) async-start(bf16[16,2,4096]{2,1,0:T(2,128)(2,1)} %reshape.219), calls=%async_computation.3 | async-start | bytes 524288 | tf_op jit(solution)/shard_map/all_to_all | solution.py:101
  558.1 4.7 copy-start.7
  558.1 44.0 %all-to-all-start.2 = ((bf16[16,48,1536]{2,1,0:T(8,128)(2,1)}), bf16[16,48,1536]{2,1,0:T(8,128)(2,1)S(1)}, u32[]{:S(2)}, u32[]{:S(2)}) async-start(bf16[16,48,1536]{2,1,0:T(8,128)(2,1)} %bitcast.93), calls=%async_computation.2 | async-start | bytes 4718592 | tf_op jit(solution)/shard_map/all_to_all | solution.py:158
  602.2 1.4 copy-start.1
  607.9 4.5 copy-start.3
Sparse Core Ops, SparseCore 0:
  11.9 151.0 all-gather.3
  215.3 111.8 all-gather.5
where the time goes:
time: 621 us; the launch traced here: 620 us
  waiting for transfers between devices  450 us (72%)
  starting transfers between devices  49.5 us (8%)
  blocking collectives  43.4 us (7%)
  local copies, waits for them, and re-layouts  24.9 us (4%)
  matrix products  23.5 us (4%)
  between operations  14.4 us (2%)
  other arithmetic  11.5 us (2%)
    all_gather x1, waiting for transfers between devices, body(): lax.all_gather(normed_in, 'tp', axis=0, tiled=True)  153 us
    all_to_all x1, waiting for transfers between devices, body(): lax.all_to_all(send_buf, 'tp', split_axis=0, concat_axis=0, tiled=True)  109 us
    all_to_all x1, waiting for transfers between devices, body(): lax.all_to_all(ordered_pages, 'tp', split_axis=0, concat_axis=2, tiled=True)  85 us
    all_gather x1, waiting for transfers between devices, body(): lax.all_gather(w_out, 'tp', axis=0, tiled=True)  55.3 us
    all_gather x1, blocking collectives, body(): seg_all = lax.all_gather(segment_ids, 'tp', axis=0, tiled=True)  43.4 us
    all_to_all x1, waiting for transfers between devices, body(): lax.all_to_all(half_out, 'tp', split_axis=0, concat_axis=0, tiled=True)  33.7 us
    all_to_all x1, starting transfers between devices, body(): lax.all_to_all(attended, 'tp', split_axis=0, concat_axis=1, tiled=True)  20.4 us
    ppermute x3, waiting for transfers between devices, from_behind(): return lax.ppermute(block, axis, route)  14.1 us
  transfers between devices with their start and end apart: 10, of which 8 were waited for; matrix products, arithmetic and copies ran while one was open for 5% of the time, Pallas kernels for 0%

commit v1 on v0

--- a/solution.py
+++ b/solution.py
@@ -1,3 +1,4 @@
+import functools
 import jax
 import jax.numpy as jnp
 from jax import lax
@@ -5,6 +6,21 @@
 
 HEAD_SIZE = 64
 PAGE = 16
+
+
+def chunk_divide(sheet, a_name):
+    return jnp.concatenate(
+        lax.all_to_all(
+            jnp.stack(lax.axis_size(a_name) * [sheet], 0),
+            axis_name=a_name,
+            split_axis=0,
+            concat_axis=0,
+        ),
+        0,
+    )
+
+
+_shape_series = functools.partial(chunk_divide, a_name="tp")
 
 
 def partner_2(block, axis, bit):
@@ -84,9 +100,7 @@
     normed_in = rms_scale(tokens, attn_gain)
     both_cols = jnp.concatenate([w_query, key_value_weight], axis=1)
     projected = jnp.dot(
-        lax.all_gather(normed_in, "tp", axis=0, tiled=True),
-        both_cols,
-        preferred_element_type=jnp.float32,
+        _shape_series(normed_in), both_cols, preferred_element_type=jnp.float32
     ).astype(jnp.bfloat16)
     group_tok = projected.shape[0]
     query_rows = projected[:, :head_cols].reshape(group_tok, heads_here, HEAD_SIZE)

time: 621 us -> 748 us (1.20)
  the two profiles are of different devices: /device:TPU:103 before, /device:TPU:207 now
where the time goes in v1:
time: 748 us; the launch traced here: 747 us
  blocking collectives  330 us (44%)
  waiting for transfers between devices  293 us (39%)
  starting transfers between devices  49.4 us (7%)
  local copies, waits for them, and re-layouts  25.5 us (3%)
  matrix products  20.7 us (3%)
  between operations  14.4 us (2%)
  other arithmetic  10.8 us (1%)
    all_to_all x1, blocking collectives, chunk_divide(): lax.all_to_all(jnp.stack(lax.axis_size(a_name) * [sheet], 0), axis_name=a...  296 us
    all_to_all x1, waiting for transfers between devices, body(): lax.all_to_all(send_buf, 'tp', split_axis=0, concat_axis=0, tiled=True)  118 us
    all_to_all x1, waiting for transfers between devices, body(): lax.all_to_all(half_out, 'tp', split_axis=0, concat_axis=0, tiled=True)  95.6 us
    all_gather x1, waiting for transfers between devices, body(): lax.all_gather(w_out, 'tp', axis=0, tiled=True)  55.2 us
    all_gather x1, blocking collectives, body(): seg_all = lax.all_gather(segment_ids, 'tp', axis=0, tiled=True)  33.7 us
    ppermute x3, waiting for transfers between devices, from_behind(): return lax.ppermute(block, axis, route)  16.7 us
    all_to_all x1, starting transfers between devices, body(): lax.all_to_all(attended, 'tp', split_axis=0, concat_axis=1, tiled=True)  15.9 us
  transfers between devices with their start and end apart: 9, of which 7 were waited for; matrix products, arithmetic and copies ran while one was open for 4% of the time, Pallas kernels for 0%

profile of v1, /device:TPU:207, one launch (start us, length us, event | category | flops | bytes accessed | tf_op | source)
XLA Modules:
  0.0 746.6 jit_solution(5129356998474854661)
XLA Ops:
  7.2 1.2 fusion.17
  8.5 1.2 fusion.19
  9.6 0.6 stack.2
  10.3 296.4 %all_to_all.52 = bf16[16,128,1536]{2,1,0:T(8,128)(2,1)S(1)} all-to-all(bf16[16,128,1536]{2,1,0:T(8,128)(2,1)S(1)} %stack.2), channel_id=1, replica_groups=mesh['grp'=32,'tp'=16] {'tp'}, dimensions={0} | all-to-all | bytes 12582912 | tf_op jit(solution)/shard_map/all_to_all | solution.py:13
  306.6 2.1 convolution_convert_fusion.2
  308.8 3.3 collective-permute-start
  312.1 33.7 %all-gather = s32[16,1,128]{2,1,0:T(1,128)S(1)} all-gather(s32[1,1,128]{2,1,0:T(1,128)S(1)} %bitcast.104), channel_id=1, replica_groups=mesh['grp'=32,'tp'=16] {'tp'}, dimensions={0}, use_global_device_ids=true | all-gather | bytes 8704 | tf_op jit(solution)/shard_map/all_gather | solution.py:116
  345.8 6.2 collective-permute-start.2
  352.1 1.9 collective-permute-start.3
  354.0 7.4 collective-permute-done.2
  361.4 3.7 collective-permute-start.1
  365.1 3.8 collective-permute-done.3
  368.9 5.6 collective-permute-done.1
  374.6 15.4 %while.12 = (s32[]{:T(128)}, bf16[4,512,1,64]{1,3,2,0:T(8,128)(2,1)S(1)}, s32[4]{0:T(128)S(1)}, bf16[4096,1,64]{0,2,1:T(8,128)(2,1)S(1)}, s32[2048]{0:T(1024)S(1...) while((s32[]{:T(128)}, ...), condition=%wide.region_4.5_spmd, body=%wide.region_1.4_spmd.sunk | while | flops 210011136 | bytes 10017057 | solution.py:77
  376.0 1.0 fusion.54
  377.6 0.8 fusion.56
  379.8 1.0 fusion.54
  381.4 0.8 fusion.56
  383.7 1.0 fusion.54
  385.3 0.8 fusion.56
  387.5 1.0 fusion.54
  389.1 0.8 fusion.56
  390.3 0.8 copy.44
  391.1 15.9 %all-to-all-start.1 = ((bf16[16,128,64]{1,2,0:T(8,128)(2,1)}), bf16[16,128,64]{1,2,0:T(8,128)(2,1)S(1)}, u32[]{:S(2)}, u32[]{:S(2)}) async-start(bf16[16,128,64]{1,2,0:T(8,128)(2,1)} %copy.44), calls=%async_computation.1 | async-start | bytes 524288 | tf_op jit(solution)/shard_map/all_to_all | solution.py:132
  408.6 55.2 %all-gather.3.cloned.1.call-done = bf16[1024,1536]{1,0:T(8,128)(2,1)} async-done(((bf16[64,1536]{1,0:T(8,128)(2,1)}), bf16[1024,1536]{1,0:T(8,128)(2,1)}) %all-gather.3.cloned.1.call-update) | async-done | bytes 3145744 | tf_op jit(solution)/shard_map/all_gather | solution.py:135
  463.9 2.6 multiply_reduce_fusion.1
  466.5 0.9 copy-done.2
  467.9 1.6 broadcast_in_dim.43
  469.5 4.6 all-to-all-start.2
  474.2 1.0 copy.52
  475.2 2.5 gather_fusion.1
  477.8 2.1 reshape.225
  479.9 118.4 %all-to-all-done.2 = bf16[16,48,1536]{2,1,0:T(8,128)(2,1)S(1)} async-done(((bf16[16,48,1536]{2,1,0:T(8,128)(2,1)}), bf16[16,48,1536]{2,1,0:T(8,128)(2,1)S(1)}, u32[]{:S(2)}, u32[]{:S(2)}) %all-to-all-start.2) | async-done | bytes 2359328 | tf_op jit(solution)/shard_map/all_to_all | solution.py:164
  598.4 6.3 all-to-all-start.4
  604.7 2.8 fusion.40
  607.5 5.3 convolution_convert_fusion
  612.8 7.0 all-to-all-done.4
  619.7 7.6 %all-to-all-start.3 = ((bf16[16,48,1536]{2,1,0:T(8,128)(2,1)}), bf16[16,48,1536]{2,1,0:T(8,128)(2,1)S(1)}, u32[]{:S(2)}, u32[]{:S(2)}) async-start(bf16[16,48,1536]{2,1,0:T(8,128)(2,1)} %bitcast.95), calls=%async_computation.3 | async-start | bytes 4718592 | tf_op jit(solution)/shard_map/all_to_all | solution.py:172
  627.6 1.2 reshape.226
  628.8 2.2 copy.53
  631.0 2.1 all_to_all.46
  633.1 95.6 %all-to-all-done.3 = bf16[16,48,1536]{2,1,0:T(8,128)(2,1)S(1)} async-done(((bf16[16,48,1536]{2,1,0:T(8,128)(2,1)}), bf16[16,48,1536]{2,1,0:T(8,128)(2,1)S(1)}, u32[]{:S(2)}, u32[]{:S(2)}) %all-to-all-start.3) | async-done | bytes 2359328 | tf_op jit(solution)/shard_map/all_to_all | solution.py:172
  728.8 1.4 copy-done.1
  730.2 1.9 convert_add_fusion
  732.1 2.3 gather_fusion
  734.5 2.3 reshape.204
  736.8 2.2 multiply_reduce_fusion
  739.0 0.8 add_convert_fusion
  (83 shorter events, 8.5 us)
Async XLA Ops:
  7.2 600.3 %copy-start = (bf16[256,1536]{1,0:T(8,128)(2,1)S(1)}, bf16[256,1536]{1,0:T(8,128)(2,1)}, u32[]{:S(2)}) copy-start(bf16[256,1536]{1,0:T(8,128)(2,1)} %param.26) | copy-start | bytes 2359300
  7.2 456.7 %all-gather.3.cloned.1.call-start = ((), (), s32[]{:S(2)}) async-start(), calls=%async_computation.5 | async-start | bytes 3342336 | tf_op jit(solution)/shard_map/all_gather | solution.py:135
  10.2 296.4 %copy-start.9 = (bf16[1536,64]{0,1:T(8,128)(2,1)S(1)}, bf16[1536,64]{0,1:T(8,128)(2,1)}, u32[]{:S(2)}) copy-start(bf16[1536,64]{0,1:T(8,128)(2,1)} %param.19) | copy-start | bytes 589828
  10.2 296.4 %copy-start.10 = (bf16[1536,64]{0,1:T(8,128)(2,1)S(1)}, bf16[1536,64]{0,1:T(8,128)(2,1)}, u32[]{:S(2)}) copy-start(bf16[1536,64]{0,1:T(8,128)(2,1)} %param.18) | copy-start | bytes 589828
  306.6 5.4 copy-start.8
  308.8 43.3 %collective-permute-start = (bf16[2048,64]{0,1:T(8,128)(2,1)S(1)}, bf16[2048,64]{0,1:T(8,128)(2,1)S(1)}, u32[]{:S(2)}, u32[]{:S(2)}) collective-permute-start(bf16[2048,64]{0,1:T(8,128)(2,1)S(1)} %slice.28), channel_id=1, source_target_pairs={{0,8},{8,0},{1,9},{9,1},{2,10},{10,2},{3,11},{11,3},{4,12},{12,4},... | collective-permute-start | bytes 786440 | tf_op jit(solution)/shard_map/ppermute | solution.py:33
  345.8 15.6 %collective-permute-start.2 = (s32[2048]{0:T(1024)S(1)}, s32[2048]{0:T(1024)S(1)}, u32[]{:S(2)}, u32[]{:S(2)}) collective-permute-start(s32[2048]{0:T(1024)S(1)} %bitcast.99), channel_id=1, source_target_pairs={{0,16},{16,32},{32,48},{48,64},{64,80},{80,96},{96,112},{112,128},... | collective-permute-start | bytes 24584 | tf_op jit(solution)/shard_map/ppermute | solution.py:39
  352.1 16.8 %collective-permute-start.3 = (bf16[2048,64]{0,1:T(8,128)(2,1)S(1)}, bf16[2048,64]{0,1:T(8,128)(2,1)S(1)}, u32[]{:S(2)}, u32[]{:S(2)}) collective-permute-start(bf16[2048,64]{0,1:T(8,128)(2,1)S(1)} %get-tuple-element.131), channel_id=1, source_target_pairs={{0,16},{16,32},{32,48},{48,64},{64,80},{80,96},{96,112},{112,128},... | collective-permute-start | bytes 786440 | tf_op jit(solution)/shard_map/ppermute | solution.py:39
  361.4 13.1 %collective-permute-start.1 = (bf16[2048,64]{0,1:T(8,128)(2,1)S(1)}, bf16[2048,64]{0,1:T(8,128)(2,1)S(1)}, u32[]{:S(2)}, u32[]{:S(2)}) collective-permute-start(bf16[2048,64]{0,1:T(8,128)(2,1)S(1)} %get-tuple-element.132), channel_id=1, source_target_pairs={{0,16},{16,32},{32,48},{48,64},{64,80},{80,96},{96,112},{112,128},... | collective-permute-start | bytes 786440 | tf_op jit(solution)/shard_map/ppermute | solution.py:39
  374.5 32.4 %copy-start.6 = (s32[128,2]{0,1:T(2,128)S(1)}, s32[128,2]{0,1:T(2,128)}, u32[]{:S(2)}) copy-start(s32[128,2]{0,1:T(2,128)} %param.22) | copy-start | bytes 3076
  390.0 73.9 %copy-start.4 = (bf16[128,1536]{1,0:T(8,128)(2,1)S(1)}, bf16[128,1536]{1,0:T(8,128)(2,1)}, u32[]{:S(2)}) copy-start(bf16[128,1536]{1,0:T(8,128)(2,1)} %param.15) | copy-start | bytes 1179652
  391.1 72.8 %all-to-all-start.1 = ((bf16[16,128,64]{1,2,0:T(8,128)(2,1)}), bf16[16,128,64]{1,2,0:T(8,128)(2,1)S(1)}, u32[]{:S(2)}, u32[]{:S(2)}) async-start(bf16[16,128,64]{1,2,0:T(8,128)(2,1)} %copy.44), calls=%async_computation.1 | async-start | bytes 524288 | tf_op jit(solution)/shard_map/all_to_all | solution.py:132
  408.5 58.8 %copy-start.5 = (f32[1536]{0:T(1024)S(1)}, f32[1536]{0:T(1024)}, u32[]{:S(2)}) copy-start(f32[1536]{0:T(1024)} %param.17) | copy-start | bytes 18436
  466.4 0.9 copy-start.2
  469.5 4.6 copy-start.11
  469.5 128.8 %all-to-all-start.2 = ((bf16[16,48,1536]{2,1,0:T(8,128)(2,1)}), bf16[16,48,1536]{2,1,0:T(8,128)(2,1)S(1)}, u32[]{:S(2)}, u32[]{:S(2)}) async-start(bf16[16,48,1536]{2,1,0:T(8,128)(2,1)} %bitcast.18), calls=%async_computation.2 | async-start | bytes 4718592 | tf_op jit(solution)/shard_map/all_to_all | solution.py:164
  598.4 21.4 %all-to-all-start.4 = ((bf16[16,2,4096]{2,1,0:T(2,128)(2,1)}), bf16[16,2,4096]{2,1,0:T(2,128)(2,1)S(1)}, u32[]{:S(2)}, u32[]{:S(2)}) async-start(bf16[16,2,4096]{2,1,0:T(2,128)(2,1)} %reshape.225), calls=%async_computation.4 | async-start | bytes 524288 | tf_op jit(solution)/shard_map/all_to_all | solution.py:115
  619.7 7.7 %copy-start.7 = (f32[128,2]{0,1:T(2,128)S(1)}, f32[128,2]{0,1:T(2,128)}, u32[]{:S(2)}) copy-start(f32[128,2]{0,1:T(2,128)} %param.23) | copy-start | bytes 3076
  619.7 109.0 %all-to-all-start.3 = ((bf16[16,48,1536]{2,1,0:T(8,128)(2,1)}), bf16[16,48,1536]{2,1,0:T(8,128)(2,1)S(1)}, u32[]{:S(2)}, u32[]{:S(2)}) async-start(bf16[16,48,1536]{2,1,0:T(8,128)(2,1)} %bitcast.95), calls=%async_computation.3 | async-start | bytes 4718592 | tf_op jit(solution)/shard_map/all_to_all | solution.py:172
  728.7 1.4 copy-start.1
  734.4 4.5 copy-start.3
Sparse Core Ops, SparseCore 0:
  352.1 111.6 all-gather.2
